TPU v7x, 32 devices: a whole 2x2x4 slice. The times are simulated.
32 devices in a mesh: dp: 8 (over z, x), space: 4 (over y, core).
Axes of the slice: x: 2, y: 2, z: 4, core: 2. Of those that a mesh axis runs over, the one named last changes fastest.
Arguments:
- images: bfloat16 [256, 24, 24, 384], P('dp', 'space'), may hold values from -6 to 6
- cotangent: bfloat16 [256, 24, 24, 384], P('dp', 'space'), may hold values from -6 to 6
- image_sides: int32 [256], P('dp'), may hold values from 14 to 24, as said below
- keep_flags: int32 [256], P('dp'), may hold values 0 or 1
- depth_kernel: float32 [49, 384], P(None, ('dp', 'space')), may hold values from -0.875 to 0.875
- kernel_moment: float32 [49, 384], P(None, ('dp', 'space')), may hold values from -0.00061035156 to 0.00061035156
- kernel_square: float32 [49, 384], P(None, ('dp', 'space')), may hold values from 4.1600107e-10 to 6.656017e-09
- block_vectors: float32 [5, 384], P(None, ('dp', 'space')), may hold values from -1.5 to 1.5
- vector_moment: float32 [5, 384], P(None, ('dp', 'space')), may hold values from -0.00061035156 to 0.00061035156
- vector_square: float32 [5, 384], P(None, ('dp', 'space')), may hold values from 4.1600107e-10 to 6.656017e-09
- up_weight: float32 [384, 1536], P(None, ('dp', 'space')), may hold values from -0.3125 to 0.3125
- up_moment: float32 [384, 1536], P(None, ('dp', 'space')), may hold values from -0.00061035156 to 0.00061035156
- up_square: float32 [384, 1536], P(None, ('dp', 'space')), may hold values from 4.1600107e-10 to 6.656017e-09
- up_bias: float32 [1536], P(('dp', 'space')), may hold values from -3 to 3
- bias_moment: float32 [1536], P(('dp', 'space')), may hold values from -0.00061035156 to 0.00061035156
- bias_square: float32 [1536], P(('dp', 'space')), may hold values from 4.1600107e-10 to 6.656017e-09
- down_weight: float32 [1536, 384], P(('dp', 'space')), may hold values from -0.15625 to 0.15625
- down_moment: float32 [1536, 384], P(('dp', 'space')), may hold values from -0.00061035156 to 0.00061035156
- down_square: float32 [1536, 384], P(('dp', 'space')), may hold values from 4.1600107e-10 to 6.656017e-09
Outputs:
- out_images: bfloat16 [256, 24, 24, 384], P('dp', 'space')
- grad_images: bfloat16 [256, 24, 24, 384], P('dp', 'space')
- new_kernel: float32 [49, 384], P(None, ('dp', 'space'))
- new_kernel_moment: float32 [49, 384], P(None, ('dp', 'space'))
- new_kernel_square: float32 [49, 384], P(None, ('dp', 'space'))
- new_vectors: float32 [5, 384], P(None, ('dp', 'space'))
- new_vector_moment: float32 [5, 384], P(None, ('dp', 'space'))
- new_vector_square: float32 [5, 384], P(None, ('dp', 'space'))
- new_up: float32 [384, 1536], P(None, ('dp', 'space'))
- new_up_moment: float32 [384, 1536], P(None, ('dp', 'space'))
- new_up_square: float32 [384, 1536], P(None, ('dp', 'space'))
- new_bias: float32 [1536], P(('dp', 'space'))
- new_bias_moment: float32 [1536], P(('dp', 'space'))
- new_bias_square: float32 [1536], P(('dp', 'space'))
- new_down: float32 [1536, 384], P(('dp', 'space'))
- new_down_moment: float32 [1536, 384], P(('dp', 'space'))
- new_down_square: float32 [1536, 384], P(('dp', 'space'))
- grad_norm: float32 [], replicated
Inputs may be any that keep to these rules, and one draw needn't show every extreme that they name: `image_sides`: each image's valid square has one of the sides 24, 18, 14.
All inputs are finite; a program needn't handle non-finite values. No bound on the sum of `keep_flags` on one device may be relied on, other than what follows from the above.
Results may differ from a plain program's by a relative error of at most 0.0055.
Values may be sent and summed in bfloat16 or wider, within the bound.
No kernel may reach another device: no remote copies, remote signals or barrier semaphores. Data moves between devices by JAX's collectives and lax.ppermute only.
A program may use at most 192 MiB of HBM per device.

v0:
```python
import jax
import jax.numpy as jnp
from jax import lax
from jax.sharding import PartitionSpec as P

STEP = 5
keep_scale = 4.0 / 3.0
norm_eps = 1e-06
clip_limit = 1.0
beta_one = 0.9
beta_two = 0.999
adam_eps = 1e-08
decay_rate = 0.05
step_rates = (0.15, 0.5, 0.05, 0.2, 0.025)
inv_root_two = 0.7071067811865476
inv_root_tau = 0.3989422804014327


def conv_rows(padded, kernel, out_rows, out_cols):
    wide = jnp.pad(padded, ((0, 0), (0, 0), (3, 3), (0, 0)))
    running = jnp.zeros((padded.shape[0], out_rows, out_cols, padded.shape[3]), jnp.float32)
    for row_off in range(7):
        for col_off in range(7):
            running = (
                running
                + kernel[row_off * 7 + col_off]
                * wide[:, row_off : row_off + out_rows, col_off : col_off + out_cols, :]
            )
    return running


def kernel_grad(padded, grad_conv):
    wide = jnp.pad(padded, ((0, 0), (0, 0), (3, 3), (0, 0)))
    out_rows = grad_conv.shape[1]
    out_cols = grad_conv.shape[2]
    pieces = [
        jnp.sum(
            wide[:, row_off : row_off + out_rows, col_off : col_off + out_cols, :] * grad_conv,
            axis=(0, 1, 2),
        )
        for row_off in range(7)
        for col_off in range(7)
    ]
    return jnp.stack(pieces)


def adam_update(weight, moment, square, grad_part, factor, step_rate):
    scaled = grad_part * factor
    new_moment = beta_one * moment + (1.0 - beta_one) * scaled
    new_square = beta_two * square + (1.0 - beta_two) * scaled * scaled
    corrected = new_moment / (1.0 - beta_one**STEP)
    spread = jnp.sqrt(new_square / (1.0 - beta_two**STEP))
    new_weight = weight - step_rate * (corrected / (spread + adam_eps) + decay_rate * weight)
    return (new_weight, new_moment, new_square)


def body(
    images,
    cotangent,
    image_sides,
    keep_flags,
    depth_kernel,
    kernel_moment,
    kernel_square,
    block_vectors,
    vector_moment,
    vector_square,
    up_weight,
    up_moment,
    up_square,
    up_bias,
    bias_moment,
    bias_square,
    down_weight,
    down_moment,
    down_square,
):
    up_full, down_full = (
        lax.all_gather(up_weight.astype(jnp.bfloat16), ("dp", "space"), axis=1, tiled=True),
        lax.all_gather(down_weight.astype(jnp.bfloat16), ("dp", "space"), axis=0, tiled=True),
    )
    kernel_full, vector_full, bias_full = (
        lax.all_gather(depth_kernel, ("dp", "space"), axis=1, tiled=True),
        lax.all_gather(block_vectors, ("dp", "space"), axis=1, tiled=True),
        lax.all_gather(up_bias, ("dp", "space"), axis=0, tiled=True),
    )
    map_side = images.shape[2]
    local_images, local_cot = (
        lax.all_to_all(images, "space", split_axis=0, concat_axis=1, tiled=True),
        lax.all_to_all(cotangent, "space", split_axis=0, concat_axis=1, tiled=True),
    )
    img_count = local_images.shape[0]
    first_image = lax.axis_index("space") * img_count
    local_sides = lax.dynamic_slice_in_dim(image_sides, first_image, img_count)
    local_keep = lax.dynamic_slice_in_dim(keep_flags, first_image, img_count)
    row_ids = jnp.arange(map_side, dtype=jnp.int32)
    col_ids = jnp.arange(map_side, dtype=jnp.int32)
    rows_in = row_ids[None, :] < local_sides[:, None]
    cols_in = col_ids[None, :] < local_sides[:, None]
    pixel_mask = (rows_in[:, :, None] & cols_in[:, None, :]).astype(jnp.float32)
    branch_scale = pixel_mask * (local_keep.astype(jnp.float32) * keep_scale)[:, None, None]
    masked = local_images * pixel_mask.astype(jnp.bfloat16)[..., None]
    padded = jnp.pad(masked, ((0, 0), (3, 3), (0, 0), (0, 0)))
    out_rows = local_images.shape[1]
    conv = conv_rows(padded, kernel_full, out_rows, map_side) + vector_full[0]
    chan_mean = jnp.mean(conv, axis=-1, keepdims=True)
    centred = conv - chan_mean
    chan_var = jnp.mean(centred * centred, axis=-1, keepdims=True)
    inv_std = lax.rsqrt(chan_var + norm_eps)
    unit_norm = centred * inv_std
    normed = (unit_norm * vector_full[1] + vector_full[2]).astype(jnp.bfloat16)
    hidden = (
        jnp.einsum("nijc,ch->nijh", normed, up_full, preferred_element_type=jnp.float32) + bias_full
    )
    normal_cdf = 0.5 * (1.0 + lax.erf(hidden * inv_root_two))
    active = (hidden * normal_cdf).astype(jnp.bfloat16)
    branch = (
        jnp.einsum("nijh,hc->nijc", active, down_full, preferred_element_type=jnp.float32)
        + vector_full[3]
    )
    out_images = (
        local_images.astype(jnp.float32) + branch_scale[..., None] * vector_full[4] * branch
    ).astype(jnp.bfloat16)
    grad_out = local_cot.astype(jnp.float32)
    grad_branch = (grad_out * branch_scale[..., None] * vector_full[4]).astype(jnp.bfloat16)
    grad_scale = jnp.sum(grad_out * branch_scale[..., None] * branch, axis=(0, 1, 2))
    grad_outbias = jnp.sum(grad_branch.astype(jnp.float32), axis=(0, 1, 2))
    grad_down = jnp.einsum("nijh,nijc->hc", active, grad_branch, preferred_element_type=jnp.float32)
    grad_active = jnp.einsum(
        "nijc,hc->nijh", grad_branch, down_full, preferred_element_type=jnp.float32
    )
    slope = normal_cdf + hidden * inv_root_tau * jnp.exp(-0.5 * hidden * hidden)
    grad_hidden = (grad_active * slope).astype(jnp.bfloat16)
    grad_up = jnp.einsum("nijc,nijh->ch", normed, grad_hidden, preferred_element_type=jnp.float32)
    grad_upbias = jnp.sum(grad_hidden.astype(jnp.float32), axis=(0, 1, 2))
    grad_normed = jnp.einsum(
        "nijh,ch->nijc", grad_hidden, up_full, preferred_element_type=jnp.float32
    )
    grad_gain = jnp.sum(grad_normed * unit_norm, axis=(0, 1, 2))
    grad_shift = jnp.sum(grad_normed, axis=(0, 1, 2))
    scaled_dn = grad_normed * vector_full[1]
    grad_conv = inv_std * (
        scaled_dn
        - jnp.mean(scaled_dn, axis=-1, keepdims=True)
        - unit_norm * jnp.mean(scaled_dn * unit_norm, axis=-1, keepdims=True)
    )
    grad_convbias = jnp.sum(grad_conv, axis=(0, 1, 2))
    grad_rows = jnp.pad(grad_conv, ((0, 0), (3, 3), (0, 0), (0, 0)))
    grad_u = conv_rows(grad_rows, kernel_full[::-1], out_rows, map_side)
    grad_local = (grad_out + pixel_mask[..., None] * grad_u).astype(jnp.bfloat16)
    grad_kernel = kernel_grad(padded, grad_conv)
    grad_vectors = jnp.stack([grad_convbias, grad_gain, grad_shift, grad_outbias, grad_scale])
    out_tiles, grad_tiles = (
        lax.all_to_all(out_images, "space", split_axis=1, concat_axis=0, tiled=True),
        lax.all_to_all(grad_local, "space", split_axis=1, concat_axis=0, tiled=True),
    )
    local_grads = (grad_kernel, grad_vectors, grad_up, grad_upbias, grad_down)
    summed = lax.psum(
        (local_grads[0], local_grads[1], local_grads[2], local_grads[3], local_grads[4]),
        ("dp", "space"),
    )
    total_squares = sum((jnp.sum(g * g) for g in summed))
    owner = lax.axis_index(("dp", "space"))
    shard_grads = (
        lax.dynamic_slice_in_dim(
            summed[0], owner * depth_kernel.shape[1], depth_kernel.shape[1], 1
        ),
        lax.dynamic_slice_in_dim(
            summed[1], owner * block_vectors.shape[1], block_vectors.shape[1], 1
        ),
        lax.dynamic_slice_in_dim(summed[2], owner * up_weight.shape[1], up_weight.shape[1], 1),
        lax.dynamic_slice_in_dim(summed[3], owner * up_bias.shape[0], up_bias.shape[0], 0),
        lax.dynamic_slice_in_dim(summed[4], owner * down_weight.shape[0], down_weight.shape[0], 0),
    )
    grad_norm = jnp.sqrt(total_squares)
    factor = clip_limit / jnp.maximum(grad_norm, clip_limit)
    states = (
        (depth_kernel, kernel_moment, kernel_square),
        (block_vectors, vector_moment, vector_square),
        (up_weight, up_moment, up_square),
        (up_bias, bias_moment, bias_square),
        (down_weight, down_moment, down_square),
    )
    results = []
    for (weight, moment, square), grad_part, step_rate in zip(states, shard_grads, step_rates):
        results.extend(adam_update(weight, moment, square, grad_part, factor, step_rate))
    return (
        out_tiles,
        grad_tiles,
        results[0],
        results[1],
        results[2],
        results[3],
        results[4],
        results[5],
        results[6],
        results[7],
        results[8],
        results[9],
        results[10],
        results[11],
        results[12],
        results[13],
        results[14],
        grad_norm,
    )


def solution(mesh):
    in_specs = (
        P("dp", "space", None, None),
        P("dp", "space", None, None),
        P("dp"),
        P("dp"),
        P(None, ("dp", "space")),
        P(None, ("dp", "space")),
        P(None, ("dp", "space")),
        P(None, ("dp", "space")),
        P(None, ("dp", "space")),
        P(None, ("dp", "space")),
        P(None, ("dp", "space")),
        P(None, ("dp", "space")),
        P(None, ("dp", "space")),
        P(("dp", "space")),
        P(("dp", "space")),
        P(("dp", "space")),
        P(("dp", "space"), None),
        P(("dp", "space"), None),
        P(("dp", "space"), None),
    )
    out_specs = (
        P("dp", "space", None, None),
        P("dp", "space", None, None),
        P(None, ("dp", "space")),
        P(None, ("dp", "space")),
        P(None, ("dp", "space")),
        P(None, ("dp", "space")),
        P(None, ("dp", "space")),
        P(None, ("dp", "space")),
        P(None, ("dp", "space")),
        P(None, ("dp", "space")),
        P(None, ("dp", "space")),
        P(("dp", "space")),
        P(("dp", "space")),
        P(("dp", "space")),
        P(("dp", "space"), None),
        P(("dp", "space"), None),
        P(("dp", "space"), None),
        P(),
    )
    return jax.shard_map(body, mesh=mesh, in_specs=in_specs, out_specs=out_specs, check_vma=False)
```

profile of v0, /device:TPU:12, one launch (start us, length us, event | category | flops | bytes accessed | tf_op | source)
XLA Modules:
  0.0 850.3 jit_solution(6092713917045323219)
XLA Ops:
  7.2 4.4 all-to-all-start
  13.1 38.7 %all-to-all-done = bf16[32,6,24,384]{3,2,1,0:T(8,128)(2,1)S(1)} async-done(((bf16[32,6,24,384]{3,2,1,0:T(8,128)(2,1)}), bf16[32,6,24,384]{3,2,1,0:T(8,128)(2,1)S(1)}, u32[]{:S(2)}, u32[]{:S(2)}) %all-to-all-start) | async-done | bytes 3538976 | tf_op jit(solution)/shard_map/all_to_all | solution.py:89
  51.9 6.4 all-to-all-start.2
  59.8 64.6 %all-gather = f32[32,12,5]{1,2,0:T(8,128)S(1)} all-gather(f32[1,12,5]{1,2,0:T(8,128)S(1)} %bitcast.83), channel_id=1, replica_groups=mesh['dp'=8,'space'=4] {'dp','space'}, dimensions={0}, use_global_device_ids=true | all-gather | bytes 7920 | tf_op jit(solution)/shard_map/all_gather | solution.py:84
  126.6 43.0 %all-gather.1 = f32[32,12,49]{2,1,0:T(8,128)} all-gather(f32[1,12,49]{2,1,0:T(8,128)S(1)} %bitcast.81), channel_id=1, replica_groups=mesh['dp'=8,'space'=4] {'dp','space'}, dimensions={0}, use_global_device_ids=true | all-gather | bytes 77616 | tf_op jit(solution)/shard_map/all_gather | solution.py:83
  171.6 45.5 %all-reduce.4 = f32[1536]{0:T(1024)} all-reduce(f32[1536]{0:T(1024)S(1)} %dynamic-update-slice), channel_id=1, replica_groups=mesh['dp'=8,'space'=4] {'dp','space'}, use_global_device_ids=true, to_apply=%add.4 | all-reduce | flops 1536 | bytes 12288
  221.4 2.6 slice_reduce_fusion.47
  224.0 2.6 slice_reduce_fusion.48
  229.4 5.5 copy.165
  238.3 59.4 %fusion.231 = (f32[8,24,24]{2,1,0:T(8,128)S(1)}, f32[8,24,24,384]{3,2,1,0:T(8,128)S(1)}) fusion(f32[384]{0:T(512)} %get-tuple-element.179, f32[384]{0:T(512)S(1)} %copy-done.48, f32[384]{0:T(512)S(1)} %copy-done.49, f32[384]{0:T(512)S(1)} %copy-done.50, bf16[8,30,24,384]{3,2,1,0:T(8,128)(2,1)S(1)} %pad.17, f32[384]{0:T(512)S(1)} %copy-done.51, ...), kind=kLoop, calls=%fused_computation.507 | loop fusion | flops 267185664 | bytes 36440576 | tf_op jit(solution)/shard_map/reduce_sum | solution.py:106
  297.8 2.8 copy-done.1
  302.8 18.7 %multiply_convert_fusion = (bf16[8,24,24,1536]{3,2,1,0:T(8,128)(2,1)}, f32[8,24,24,1536]{3,2,1,0:T(8,128)}) fusion(f32[1536]{0:T(1024)S(1)} %copy-done.85, bf16[384,1536]{0,1:T(8,128)(2,1)} %all-gather.5.cloned.1.call-done, f32[8,24,24,384]{3,2,1,0:T(8,128)} %copy-done.1, f32[384]{0:T(512)} %get-tuple-element.177, f32[384]{0:T(512)S(1)} %copy-done.64, ...), kind=kOutput, calls=%fused_computation.49 | convolution fusion | flops 5487132672 | bytes 50770944 | tf_op jit(solution)/shard_map/nijc,ch->nijh/dot_general | solution.py:113
  321.5 16.5 %multiply_reduce_fusion = (f32[384]{0:T(512)}, bf16[8,24,24,384]{3,2,1,0:T(8,128)(2,1)}, bf16[8,24,24,384]{3,2,1,0:T(8,128)(2,1)S(1)}) fusion(f32[8,24,24,384]{3,2,1,0:T(8,128)} %bitcast.75, f32[384]{0:T(512)} %get-tuple-element.176, f32[8,24,24]{2,1,0:T(8,128)} %and_select_fusion.1, f32[384]{0:T(512)S(1)} %copy-done.62, ...), kind=kOutput, calls=%fused_computation.387 | convolution fusion | flops 5455281664 | bytes 33053184 | tf_op jit(solution)/shard_map/nijh,hc->nijc/dot_general | solution.py:118
  338.0 11.9 %fusion.203 = f32[1536,384]{1,0:T(8,128)} fusion(bf16[8,24,24,384]{3,2,1,0:T(8,128)(2,1)S(1)} %get-tuple-element.205, bf16[8,24,24,1536]{3,2,1,0:T(8,128)(2,1)} %get-tuple-element.208), kind=kOutput, calls=%fused_computation.401 | convolution fusion | flops 5435817984 | bytes 20054016 | tf_op jit(solution)/shard_map/nijh,nijc->hc/dot_general | solution.py:128
  349.9 21.6 %convert_reduce_fusion = (f32[1536]{0:T(1024)}, bf16[8,24,24,1536]{3,2,1,0:T(8,128)(2,1)}) fusion(f32[8,24,24,1536]{3,2,1,0:T(8,128)} %get-tuple-element.209, f32[1536]{0:T(1024)S(1)} %copy-done.85, bf16[8,24,24,384]{3,2,1,0:T(8,128)(2,1)S(1)} %get-tuple-element.205, bf16[1536,384]{1,0:T(8,128)(2,1)S(1)} %copy-done.112), kind=kOutput, calls=%fused_computation.48 | convolution fusion | flops 5527828992 | bytes 47198208 | tf_op jit(solution)/shard_map/nijc,hc->nijh/dot_general | solution.py:129
  371.5 16.5 %fusion.208 = f32[384,1536]{0,1:T(8,128)} fusion(bf16[8,24,24,1536]{3,2,1,0:T(8,128)(2,1)} %get-tuple-element.212, f32[8,24,24,384]{3,2,1,0:T(8,128)} %copy-done.1, f32[384]{0:T(512)S(1)} %copy-done.106, f32[384]{0:T(512)S(1)} %copy-done.64, f32[8,24,24]{2,1,0:T(8,128)S(1)} %copy-done.11, f32[8,24,24]{2,1,0:T(8,128)S(1)} %copy-done.8), kind=kOutput, calls=%fused_computation.402 | convolution fusion | flops 5444665344 | bytes 23632896 | tf_op jit(solution)/shard_map/nijc,nijh->ch/dot_general | solution.py:134
  388.0 15.5 %multiply_reduce_fusion.1 = (f32[384]{0:T(512)}, f32[8,24,24]{2,1,0:T(8,128)S(1)}, f32[8,24,24]{2,1,0:T(8,128)S(1)}, f32[384]{0:T(512)}, f32[8,24,24,384]{3,2,1,0:T(8,128)}) fusion(f32[8,24,24,384]{3,2,1,0:T(8,128)} %copy-done.1, f32[8,24,24]{2,1,0:T(8,128)S(1)} %copy-done.11, f32[8,24,24]{2,1,0:T(8,128)S(1)} %copy-done.8, f32[384]{0:T(512)S(1)} %copy-done.64, ...), kind=kOutput, calls=%fused_computation.389 | convolution fusion | flops 5451732992 | bytes 29569536 | tf_op jit(solution)/shard_map/nijh,ch->nijc/dot_general | solution.py:136
  404.2 36.5 %fusion.105 = (f32[384]{0:T(512)}, f32[384]{0:T(512)}, f32[384]{0:T(512)}, f32[384]{0:T(512)}, f32[384]{0:T(512)}, /*index=5*/f32[384]{0:T(512)}, f32[384]{0:T(5...) fusion(bf16[8,30,24,384]{3,2,1,0:T(8,128)(2,1)} %copy-done, ...), kind=kLoop, calls=%fused_computation.291 | loop fusion | flops 107930880 | bytes 25760256 | tf_op jit(solution)/shard_map/reduce_sum | solution.py:37
  440.7 8.9 %fusion.102 = (f32[384]{0:T(512)}, f32[384]{0:T(512)}, f32[384]{0:T(512)}, f32[384]{0:T(512)}, f32[384]{0:T(512)}, /*index=5*/f32[384]{0:T(512)}, f32[384]{0:T(512)}, f32[384]{0:T(512)}) fusion(f32[8,24,24,384]{3,2,1,0:T(8,128)} %get-tuple-element.200, bf16[8,24,24,384]{3,2,1,0:T(8,128)(2,1)S(1)} %copy-done.3), kind=kLoop, calls=%fused_computation.288 | loop fusion | flops 38925312 | bytes 10629120 | tf_op jit(solution)/shard_map/reduce_sum | solution.py:37
  449.6 8.6 %fusion.40 = (f32[384]{0:T(512)}, f32[384]{0:T(512)}, f32[384]{0:T(512)}, f32[384]{0:T(512)S(1)}, f32[384]{0:T(512)S(1)}, /*index=5*/f32[384]{0:T(512)S(1)}) fusion(f32[8,24,24,384]{3,2,1,0:T(8,128)} %get-tuple-element.200, bf16[8,30,24,384]{3,2,1,0:T(8,128)(2,1)S(1)} %bitcast.71), kind=kLoop, calls=%fused_computation.226 | loop fusion | flops 31848192 | bytes 11510784 | tf_op jit(solution)/shard_map/reduce_sum | solution.py:37
  458.2 33.2 %fusion.84 = (f32[384]{0:T(512)}, f32[384]{0:T(512)}, f32[384]{0:T(512)}, f32[384]{0:T(512)}, f32[384]{0:T(512)}, /*index=5*/f32[384]{0:T(512)}, f32[384]{0:T(51...) fusion(f32[8,24,24,384]{3,2,1,0:T(8,128)} %get-tuple-element.20, ...), kind=kLoop, calls=%fused_computation.270 | loop fusion | flops 95544576 | bytes 11529216 | tf_op jit(solution)/shard_map/reduce_sum | solution.py:37
  491.8 7.1 pad.19
  529.1 9.3 %stack.217 = f32[49,384]{1,0:T(8,128)} concatenate(f32[1,384]{1,0:T(1,128)S(1)} %stack.168, f32[1,384]{1,0:T(1,128)S(1)} %stack.169, f32[1,384]{1,0:T(1,128)} %stack.170, f32[1,384]{1,0:T(1,128)} %stack.171, f32[1,384]{1,0:T(1,128)} %stack.172, f32[1,384]{1,0:T(1,128)} %stack.173, f32[1,384]{1,0:T(1,128)} %stack.174, f32[1,384]{1,0:T(1,128)} %stack.175, f32[1,384]{1,0:T(1,128)} %stack.176, ...), dimensions={0} | concatenate | bytes 150528 | tf_op jit(solution)/shard_map/stack | solution.py:44
  542.6 3.7 all-to-all-start.1
  547.1 184.0 %fusion.195 = bf16[8,24,24,384]{3,2,1,0:T(8,128)(2,1)} fusion(f32[8,24,24,384]{3,2,1,0:T(8,128)} %bitcast.76, f32[8,30,24,384]{3,2,1,0:T(8,128)} %pad.19, f32[8,24,24,384]{3,2,1,0:T(8,128)} %get-tuple-element.200, f32[8,24,24]{2,1,0:T(8,128)} %get-tuple-element.206, f32[384]{0:T(512)} %get-tuple-element.127, f32[384]{0:T(512)} %get-tuple-element.128, ...), kind=kLoop, calls=%fused_computation.381 | loop fusion | flops 176947200 | bytes 69206016 | tf_op jit(solution)/shard_map/convert_element_type | solution.py:150
  731.1 4.5 copy.166
  735.6 4.7 all-to-all-start.3
  740.4 2.6 bitcast_convert_fusion
  747.5 67.7 %all-reduce.5 = (f32[5,384]{1,0:T(8,128)}, f32[1536]{0:T(1024)}) all-reduce(f32[5,384]{1,0:T(8,128)S(1)} %stack.223, f32[1536]{0:T(1024)} %get-tuple-element.211), channel_id=1, replica_groups=mesh['dp'=8,'space'=4] {'dp','space'}, use_global_device_ids=true, to_apply=%region_60.61 | all-reduce | flops 3456 | bytes 27648 | tf_op jit(solution)/shard_map/psum | solution.py:158
  820.7 2.9 multiply_reduce_fusion.6
  824.8 2.9 multiply_reduce_fusion.5
  838.2 4.1 copy.167
  (333 shorter events, 73.6 us)
Async XLA Ops:
  7.2 52.6 %copy-start.60 = (f32[5,12]{1,0:T(8,128)S(1)}, f32[5,12]{1,0:T(8,128)}, u32[]{:S(2)}) copy-start(f32[5,12]{1,0:T(8,128)} %param.26) | copy-start | bytes 724
  7.2 119.4 %copy-start.12 = (f32[49,12]{0,1:T(8,128)S(1)}, f32[49,12]{0,1:T(8,128)}, u32[]{:S(2)}) copy-start(f32[49,12]{0,1:T(8,128)} %param.23) | copy-start | bytes 7060
  7.2 164.1 %copy-start.110 = (f32[48]{0:T(128)S(1)}, f32[48]{0:T(128)}, u32[]{:S(2)}) copy-start(f32[48]{0:T(128)} %param.32) | copy-start | bytes 580
  7.2 44.6 %all-to-all-start = ((bf16[32,6,24,384]{3,2,1,0:T(8,128)(2,1)}), bf16[32,6,24,384]{3,2,1,0:T(8,128)(2,1)S(1)}, u32[]{:S(2)}, u32[]{:S(2)}) async-start(bf16[32,6,24,384]{3,2,1,0:T(8,128)(2,1)} %param.19), calls=%async_computation | async-start | bytes 7077888 | tf_op jit(solution)/shard_map/all_to_all | solution.py:89
  11.6 291.2 %all-gather.5.cloned.1.call-start = ((), (), s32[]{:S(2)}) async-start(), calls=%async_computation.4 | async-start | bytes 1216512 | tf_op jit(solution)/shard_map/all_gather | solution.py:79
  51.9 74.8 %copy-start.4 = (bf16[32,6,24,384]{3,2,1,0:T(8,128)(2,1)}, bf16[32,6,24,384]{3,2,1,0:T(8,128)(2,1)S(1)}, u32[]{:S(2)}) copy-start(bf16[32,6,24,384]{3,2,1,0:T(8,128)(2,1)S(1)} %all-to-all-done) | copy-start | bytes 10616836
  51.9 177.5 %all-to-all-start.2 = ((bf16[32,6,24,384]{3,2,1,0:T(8,128)(2,1)}), bf16[32,6,24,384]{3,2,1,0:T(8,128)(2,1)}, u32[]{:S(2)}, u32[]{:S(2)}) async-start(bf16[32,6,24,384]{3,2,1,0:T(8,128)(2,1)} %param.20), calls=%async_computation.2 | async-start | bytes 7077888 | tf_op jit(solution)/shard_map/all_to_all | solution.py:90
  58.2 263.3 %all-gather.7.cloned.1.call-start = ((), (), s32[]{:S(2)}) async-start(), calls=%async_computation.5 | async-start | bytes 1216512 | tf_op jit(solution)/shard_map/all_gather | solution.py:80
  236.5 61.2 %copy-start = (bf16[8,30,24,384]{3,2,1,0:T(8,128)(2,1)}, bf16[8,30,24,384]{3,2,1,0:T(8,128)(2,1)S(1)}, u32[]{:S(2)}) copy-start(bf16[8,30,24,384]{3,2,1,0:T(8,128)(2,1)S(1)} %pad.17) | copy-start | bytes 13271044
  404.2 36.5 %copy-start.3 = (bf16[8,24,24,384]{3,2,1,0:T(8,128)(2,1)S(1)}, bf16[8,24,24,384]{3,2,1,0:T(8,128)(2,1)}, u32[]{:S(2)}) copy-start(bf16[8,24,24,384]{3,2,1,0:T(8,128)(2,1)} %copy-done.2) | copy-start | bytes 10616836
  491.6 28.2 %copy-start.103 = (f32[384]{0:T(512)S(1)}, f32[384]{0:T(512)}, u32[]{:S(2)}) copy-start(f32[384]{0:T(512)} %get-tuple-element.93) | copy-start | bytes 4612
  491.6 28.2 %copy-start.102 = (f32[384]{0:T(512)S(1)}, f32[384]{0:T(512)}, u32[]{:S(2)}) copy-start(f32[384]{0:T(512)} %get-tuple-element.94) | copy-start | bytes 4612
  491.6 28.8 %copy-start.101 = (f32[384]{0:T(512)S(1)}, f32[384]{0:T(512)}, u32[]{:S(2)}) copy-start(f32[384]{0:T(512)} %get-tuple-element.95) | copy-start | bytes 4612
  491.6 29.4 %copy-start.100 = (f32[384]{0:T(512)S(1)}, f32[384]{0:T(512)}, u32[]{:S(2)}) copy-start(f32[384]{0:T(512)} %get-tuple-element.96) | copy-start | bytes 4612
  491.6 29.9 %copy-start.99 = (f32[384]{0:T(512)S(1)}, f32[384]{0:T(512)}, u32[]{:S(2)}) copy-start(f32[384]{0:T(512)} %get-tuple-element.97) | copy-start | bytes 4612
  491.6 30.5 %copy-start.98 = (f32[384]{0:T(512)S(1)}, f32[384]{0:T(512)}, u32[]{:S(2)}) copy-start(f32[384]{0:T(512)} %get-tuple-element.98) | copy-start | bytes 4612
  491.6 31.1 %copy-start.97 = (f32[384]{0:T(512)S(1)}, f32[384]{0:T(512)}, u32[]{:S(2)}) copy-start(f32[384]{0:T(512)} %get-tuple-element.99) | copy-start | bytes 4612
  491.7 31.7 %copy-start.96 = (f32[384]{0:T(512)S(1)}, f32[384]{0:T(512)}, u32[]{:S(2)}) copy-start(f32[384]{0:T(512)} %get-tuple-element.100) | copy-start | bytes 4612
  491.7 32.3 %copy-start.95 = (f32[384]{0:T(512)S(1)}, f32[384]{0:T(512)}, u32[]{:S(2)}) copy-start(f32[384]{0:T(512)} %get-tuple-element.101) | copy-start | bytes 4612
  491.7 32.9 %copy-start.94 = (f32[384]{0:T(512)S(1)}, f32[384]{0:T(512)}, u32[]{:S(2)}) copy-start(f32[384]{0:T(512)} %get-tuple-element.102) | copy-start | bytes 4612
  491.7 33.4 %copy-start.93 = (f32[384]{0:T(512)S(1)}, f32[384]{0:T(512)}, u32[]{:S(2)}) copy-start(f32[384]{0:T(512)} %get-tuple-element.103) | copy-start | bytes 4612
  491.7 34.0 %copy-start.92 = (f32[384]{0:T(512)S(1)}, f32[384]{0:T(512)}, u32[]{:S(2)}) copy-start(f32[384]{0:T(512)} %get-tuple-element.104) | copy-start | bytes 4612
  491.7 34.5 %copy-start.91 = (f32[384]{0:T(512)S(1)}, f32[384]{0:T(512)}, u32[]{:S(2)}) copy-start(f32[384]{0:T(512)} %get-tuple-element.105) | copy-start | bytes 4612
  491.7 35.1 %copy-start.90 = (f32[384]{0:T(512)S(1)}, f32[384]{0:T(512)}, u32[]{:S(2)}) copy-start(f32[384]{0:T(512)} %get-tuple-element.106) | copy-start | bytes 4612
  491.7 35.7 %copy-start.89 = (f32[384]{0:T(512)S(1)}, f32[384]{0:T(512)}, u32[]{:S(2)}) copy-start(f32[384]{0:T(512)} %get-tuple-element.107) | copy-start | bytes 4612
  491.7 36.2 %copy-start.88 = (f32[384]{0:T(512)S(1)}, f32[384]{0:T(512)}, u32[]{:S(2)}) copy-start(f32[384]{0:T(512)} %get-tuple-element.108) | copy-start | bytes 4612
  491.7 36.8 %copy-start.87 = (f32[384]{0:T(512)S(1)}, f32[384]{0:T(512)}, u32[]{:S(2)}) copy-start(f32[384]{0:T(512)} %get-tuple-element.109) | copy-start | bytes 4612
  491.8 48.4 %copy-start.6 = (bf16[8,24,24,384]{3,2,1,0:T(8,128)(2,1)S(1)}, bf16[8,24,24,384]{3,2,1,0:T(8,128)(2,1)}, u32[]{:S(2)}) copy-start(bf16[8,24,24,384]{3,2,1,0:T(8,128)(2,1)} %get-tuple-element.204) | copy-start | bytes 10616836
  542.6 193.0 %all-to-all-start.1 = ((bf16[8,24,24,384]{3,2,0,1:T(8,128)(2,1)}), bf16[8,24,24,384]{3,2,0,1:T(8,128)(2,1)S(1)}, u32[]{:S(2)}, u32[]{:S(2)}) async-start(bf16[8,24,24,384]{3,2,0,1:T(8,128)(2,1)} %copy.163), calls=%async_computation.1 | async-start | bytes 7077888 | tf_op jit(solution)/shard_map/all_to_all | solution.py:154
  546.3 271.5 %all-reduce.9.cloned.1.call-start = ((), (), s32[]{:S(2)}) async-start(), calls=%async_computation.6 | async-start | bytes 9830400 | tf_op jit(solution)/shard_map/psum | solution.py:158
  735.6 102.6 %all-to-all-start.3 = ((bf16[8,24,24,384]{3,2,0,1:T(8,128)(2,1)}), bf16[8,24,24,384]{3,2,0,1:T(8,128)(2,1)}, u32[]{:S(2)}, u32[]{:S(2)}) async-start(bf16[8,24,24,384]{3,2,0,1:T(8,128)(2,1)} %copy.166), calls=%async_computation.3 | async-start | bytes 7077888 | tf_op jit(solution)/shard_map/all_to_all | solution.py:155
  743.0 86.8 %copy-start.61 = (f32[5,12]{1,0:T(8,128)S(1)}, f32[5,12]{1,0:T(8,128)}, u32[]{:S(2)}) copy-start(f32[5,12]{1,0:T(8,128)} %param.26) | copy-start | bytes 724
  (90 other events, 746.9 us)
Sparse Core Ops, SparseCore 0:
  15.9 54.4 all-gather.4
  73.9 53.8 all-gather.6
  553.3 147.8 all-reduce.8
where the time goes:
time: 862 us; the launch traced here: 850 us
  other arithmetic  362 us (42%)
  blocking collectives  221 us (26%)
  matrix products  101 us (12%)
  local copies, waits for them, and re-layouts  88.7 us (10%)
  waiting for transfers between devices  39.5 us (5%)
  between operations  19.9 us (2%)
  starting transfers between devices  19.2 us (2%)
    convert_element_type x1, other arithmetic, body(): (grad_out + pixel_mask[..., None] * grad_u).astype(jnp.bfloat16)  184 us
    reduce_sum x4, other arithmetic, kernel_grad(): jnp.sum(wide[:, row_off:row_off + out_rows, col_off:col_off + out_cols, :...  87.2 us
    psum x1, blocking collectives, body(): lax.psum((local_grads[0], local_grads[1], local_grads[2], local_grads[3],...  67.7 us
    all_gather x1, blocking collectives, body(): lax.all_gather(block_vectors, ('dp', 'space'), axis=1, tiled=True)  64.6 us
    reduce_sum x1, other arithmetic, body(): chan_mean = jnp.mean(conv, axis=-1, keepdims=True)  59.4 us
    unnamed x1, blocking collectives  45.5 us
    all_gather x1, blocking collectives, body(): lax.all_gather(depth_kernel, ('dp', 'space'), axis=1, tiled=True)  43 us
    another operation x51, local copies, waits for them, and re-layouts, kernel_grad(): return jnp.stack(pieces)  41.1 us
  transfers between devices with their start and end apart: 7, of which 1 were waited for; matrix products, arithmetic and copies ran while one was open for 38% of the time, Pallas kernels for 0%

commit v1 on v0

--- a/solution.py
+++ b/solution.py
@@ -156,8 +156,11 @@
     )
     local_grads = (grad_kernel, grad_vectors, grad_up, grad_upbias, grad_down)
     summed = lax.psum(
-        (local_grads[0], local_grads[1], local_grads[2], local_grads[3], local_grads[4]),
-        ("dp", "space"),
+        lax.psum(
+            (local_grads[0], local_grads[1], local_grads[2], local_grads[3], local_grads[4]),
+            "space",
+        ),
+        "dp",
     )
     total_squares = sum((jnp.sum(g * g) for g in summed))
     owner = lax.axis_index(("dp", "space"))

time: 862 us -> 948 us (1.100)
  waiting for transfers between devices: 39.5 us -> 154 us
  local copies, waits for them, and re-layouts: 88.7 us -> 48.9 us
    psum x1, waiting for transfers between devices: 0.01 us -> 115 us  [body(): lax.psum((local_grads[0], local_grads[1], local_grads[2], local_grads[3],...]
    another operation x51, local copies, waits for them, and re-layouts: 41.1 us -> 1.18 us  [kernel_grad(): return jnp.stack(pieces)]
    psum x0 -> x1, blocking collectives: none -> 35 us  [body(): lax.psum(lax.psum((local_grads[0], local_grads[1], local_grads[2], local_...]
    psum x1, blocking collectives: 67.7 us -> 40.6 us  [body(): lax.psum((local_grads[0], local_grads[1], local_grads[2], local_grads[3],...]
  transfers between devices with their start and end apart: 7 -> 8, of which waited for: 1 -> 2; matrix products, arithmetic and copies ran while one was open for 38% -> 34% of each run, Pallas kernels for 0% -> 0%
where the time goes in v1:
time: 948 us; the launch traced here: 932 us
  other arithmetic  358 us (38%)
  blocking collectives  229 us (24%)
  waiting for transfers between devices  154 us (16%)
  matrix products  101 us (11%)
  local copies, waits for them, and re-layouts  48.9 us (5%)
  starting transfers between devices  20.6 us (2%)
  between operations  20.5 us (2%)
    convert_element_type x1, other arithmetic, body(): (grad_out + pixel_mask[..., None] * grad_u).astype(jnp.bfloat16)  184 us
    psum x1, waiting for transfers between devices, body(): lax.psum((local_grads[0], local_grads[1], local_grads[2], local_grads[3],...  115 us
    reduce_sum x4, other arithmetic, kernel_grad(): jnp.sum(wide[:, row_off:row_off + out_rows, col_off:col_off + out_cols, :...  86 us
    all_gather x1, blocking collectives, body(): lax.all_gather(block_vectors, ('dp', 'space'), axis=1, tiled=True)  64.6 us
    reduce_sum x1, other arithmetic, body(): chan_mean = jnp.mean(conv, axis=-1, keepdims=True)  59.4 us
    unnamed x1, blocking collectives  45.5 us
    all_gather x1, blocking collectives, body(): lax.all_gather(depth_kernel, ('dp', 'space'), axis=1, tiled=True)  43 us
    psum x1, blocking collectives, body(): lax.psum((local_grads[0], local_grads[1], local_grads[2], local_grads[3],...  40.6 us
  transfers between devices with their start and end apart: 8, of which 2 were waited for; matrix products, arithmetic and copies ran while one was open for 34% of the time, Pallas kernels for 0%

profile of v1, /device:TPU:12, one launch (start us, length us, event | category | flops | bytes accessed | tf_op | source)
XLA Modules:
  0.0 931.7 jit_solution(15236781089359766736)
XLA Ops:
  7.2 4.4 all-to-all-start
  13.1 38.7 %all-to-all-done = bf16[32,6,24,384]{3,2,1,0:T(8,128)(2,1)S(1)} async-done(((bf16[32,6,24,384]{3,2,1,0:T(8,128)(2,1)}), bf16[32,6,24,384]{3,2,1,0:T(8,128)(2,1)S(1)}, u32[]{:S(2)}, u32[]{:S(2)}) %all-to-all-start) | async-done | bytes 3538976 | tf_op jit(solution)/shard_map/all_to_all | solution.py:89
  51.9 6.4 all-to-all-start.2
  59.8 64.6 %all-gather = f32[32,12,5]{1,2,0:T(8,128)S(1)} all-gather(f32[1,12,5]{1,2,0:T(8,128)S(1)} %bitcast.83), channel_id=1, replica_groups=mesh['dp'=8,'space'=4] {'dp','space'}, dimensions={0}, use_global_device_ids=true | all-gather | bytes 7920 | tf_op jit(solution)/shard_map/all_gather | solution.py:84
  126.6 43.0 %all-gather.1 = f32[32,12,49]{2,1,0:T(8,128)} all-gather(f32[1,12,49]{2,1,0:T(8,128)S(1)} %bitcast.81), channel_id=1, replica_groups=mesh['dp'=8,'space'=4] {'dp','space'}, dimensions={0}, use_global_device_ids=true | all-gather | bytes 77616 | tf_op jit(solution)/shard_map/all_gather | solution.py:83
  171.6 45.5 %all-reduce.4 = f32[1536]{0:T(1024)} all-reduce(f32[1536]{0:T(1024)S(1)} %dynamic-update-slice), channel_id=1, replica_groups=mesh['dp'=8,'space'=4] {'dp','space'}, use_global_device_ids=true, to_apply=%add.4 | all-reduce | flops 1536 | bytes 12288
  221.4 2.6 slice_reduce_fusion.47
  224.0 2.6 slice_reduce_fusion.48
  228.7 5.5 copy.165
  237.5 59.4 %fusion.231 = (f32[8,24,24]{2,1,0:T(8,128)S(1)}, f32[8,24,24,384]{3,2,1,0:T(8,128)S(1)}) fusion(f32[384]{0:T(512)} %get-tuple-element.179, f32[384]{0:T(512)S(1)} %copy-done.56, f32[384]{0:T(512)S(1)} %copy-done.57, f32[384]{0:T(512)S(1)} %copy-done.58, bf16[8,30,24,384]{3,2,1,0:T(8,128)(2,1)S(1)} %pad.17, f32[384]{0:T(512)S(1)} %copy-done.59, ...), kind=kLoop, calls=%fused_computation.507 | loop fusion | flops 267185664 | bytes 36440576 | tf_op jit(solution)/shard_map/reduce_sum | solution.py:106
  297.0 2.8 copy-done.1
  302.1 18.7 %multiply_convert_fusion = (bf16[8,24,24,1536]{3,2,1,0:T(8,128)(2,1)}, f32[8,24,24,1536]{3,2,1,0:T(8,128)}) fusion(f32[1536]{0:T(1024)S(1)} %copy-done.90, bf16[384,1536]{0,1:T(8,128)(2,1)} %all-gather.5.cloned.1.call-done, f32[8,24,24,384]{3,2,1,0:T(8,128)} %copy-done.1, f32[384]{0:T(512)} %get-tuple-element.177, f32[384]{0:T(512)S(1)} %copy-done.72, ...), kind=kOutput, calls=%fused_computation.49 | convolution fusion | flops 5487132672 | bytes 50770944 | tf_op jit(solution)/shard_map/nijc,ch->nijh/dot_general | solution.py:113
  320.8 16.5 %multiply_reduce_fusion = (f32[384]{0:T(512)}, bf16[8,24,24,384]{3,2,1,0:T(8,128)(2,1)}, bf16[8,24,24,384]{3,2,1,0:T(8,128)(2,1)S(1)}) fusion(f32[8,24,24,384]{3,2,1,0:T(8,128)} %bitcast.75, f32[384]{0:T(512)} %get-tuple-element.176, f32[8,24,24]{2,1,0:T(8,128)} %and_select_fusion.1, f32[384]{0:T(512)S(1)} %copy-done.70, ...), kind=kOutput, calls=%fused_computation.387 | convolution fusion | flops 5455281664 | bytes 33053184 | tf_op jit(solution)/shard_map/nijh,hc->nijc/dot_general | solution.py:118
  337.3 11.9 %fusion.203 = f32[1536,384]{1,0:T(8,128)} fusion(bf16[8,24,24,384]{3,2,1,0:T(8,128)(2,1)S(1)} %get-tuple-element.210, bf16[8,24,24,1536]{3,2,1,0:T(8,128)(2,1)} %get-tuple-element.213), kind=kOutput, calls=%fused_computation.401 | convolution fusion | flops 5435817984 | bytes 20054016 | tf_op jit(solution)/shard_map/nijh,nijc->hc/dot_general | solution.py:128
  349.1 21.6 %convert_reduce_fusion = (f32[1536]{0:T(1024)}, bf16[8,24,24,1536]{3,2,1,0:T(8,128)(2,1)}) fusion(f32[8,24,24,1536]{3,2,1,0:T(8,128)} %get-tuple-element.214, f32[1536]{0:T(1024)S(1)} %copy-done.90, bf16[8,24,24,384]{3,2,1,0:T(8,128)(2,1)S(1)} %get-tuple-element.210, bf16[1536,384]{1,0:T(8,128)(2,1)S(1)} %copy-done.114), kind=kOutput, calls=%fused_computation.48 | convolution fusion | flops 5527828992 | bytes 47198208 | tf_op jit(solution)/shard_map/nijc,hc->nijh/dot_general | solution.py:129
  370.7 16.5 %fusion.208 = f32[384,1536]{0,1:T(8,128)} fusion(bf16[8,24,24,1536]{3,2,1,0:T(8,128)(2,1)} %get-tuple-element.217, f32[8,24,24,384]{3,2,1,0:T(8,128)} %copy-done.1, f32[384]{0:T(512)S(1)} %copy-done.103, f32[384]{0:T(512)S(1)} %copy-done.72, f32[8,24,24]{2,1,0:T(8,128)S(1)} %copy-done.10, f32[8,24,24]{2,1,0:T(8,128)S(1)} %copy-done.8), kind=kOutput, calls=%fused_computation.402 | convolution fusion | flops 5444665344 | bytes 23632896 | tf_op jit(solution)/shard_map/nijc,nijh->ch/dot_general | solution.py:134
  387.3 15.5 %multiply_reduce_fusion.1 = (f32[384]{0:T(512)}, f32[8,24,24]{2,1,0:T(8,128)S(1)}, f32[8,24,24]{2,1,0:T(8,128)S(1)}, f32[384]{0:T(512)}, f32[8,24,24,384]{3,2,1,0:T(8,128)}) fusion(f32[8,24,24,384]{3,2,1,0:T(8,128)} %copy-done.1, f32[8,24,24]{2,1,0:T(8,128)S(1)} %copy-done.10, f32[8,24,24]{2,1,0:T(8,128)S(1)} %copy-done.8, f32[384]{0:T(512)S(1)} %copy-done.72, ...), kind=kOutput, calls=%fused_computation.389 | convolution fusion | flops 5451732992 | bytes 29569536 | tf_op jit(solution)/shard_map/nijh,ch->nijc/dot_general | solution.py:136
  403.5 36.5 %fusion.105 = (f32[384]{0:T(512)}, f32[384]{0:T(512)}, f32[384]{0:T(512)}, f32[384]{0:T(512)}, f32[384]{0:T(512)}, /*index=5*/f32[384]{0:T(512)}, f32[384]{0:T(5...) fusion(bf16[8,30,24,384]{3,2,1,0:T(8,128)(2,1)} %copy-done, ...), kind=kLoop, calls=%fused_computation.291 | loop fusion | flops 107930880 | bytes 25760256 | tf_op jit(solution)/shard_map/reduce_sum | solution.py:37
  440.0 8.9 fusion.102
  448.9 8.1 fusion.40
  457.2 32.5 %fusion.84 = (f32[384]{0:T(512)S(1)}, f32[384]{0:T(512)S(1)}, f32[384]{0:T(512)S(1)}, f32[384]{0:T(512)S(1)}, f32[384]{0:T(512)S(1)}, /*index=5*/f32[384]{0:T(51...) fusion(f32[8,24,24,384]{3,2,1,0:T(8,128)} %get-tuple-element.20, ...), kind=kLoop, calls=%fused_computation.270 | loop fusion | flops 95544576 | bytes 11529216 | tf_op jit(solution)/shard_map/reduce_sum | solution.py:37
  491.5 7.6 pad.19
  501.5 3.7 all-to-all-start.1
  505.3 115.5 %all-reduce.14.cloned.1.call-done = (f32[49,384]{0,1:T(8,128)}, f32[384,1536]{0,1:T(8,128)}, f32[1536,384]{1,0:T(8,128)}) async-done(((f32[49,384]{0,1:T(8,128)}, f32[384,1536]{0,1:T(8,128)}, f32[1536,384]{1,0:T(8,128)}), (f32[49,384]{0,1:T(8,128)}, f32[384,1536]{0,1:T(8,128)}, f32[1536,384]{1,0:T(8,128)})) %all-reduce.14.cloned.1.call-update) | async-done | bytes 4793872 | tf_op jit(solution)/shard_map/psum | solution.py:159
  620.9 184.0 %fusion.195 = bf16[8,24,24,384]{3,2,1,0:T(8,128)(2,1)} fusion(f32[8,24,24,384]{3,2,1,0:T(8,128)} %bitcast.76, f32[8,30,24,384]{3,2,1,0:T(8,128)} %pad.19, f32[8,24,24,384]{3,2,1,0:T(8,128)} %get-tuple-element.205, f32[8,24,24]{2,1,0:T(8,128)} %get-tuple-element.211, f32[384]{0:T(512)} %get-tuple-element.127, f32[384]{0:T(512)} %get-tuple-element.128, ...), kind=kLoop, calls=%fused_computation.381 | loop fusion | flops 176947200 | bytes 69206016 | tf_op jit(solution)/shard_map/convert_element_type | solution.py:150
  805.0 4.5 copy.166
  809.4 6.0 all-to-all-start.3
  822.2 40.6 %all-reduce.7 = (f32[5,384]{1,0:T(8,128)}, f32[1536]{0:T(1024)}) all-reduce(f32[5,384]{1,0:T(8,128)S(1)} %stack.223, f32[1536]{0:T(1024)} %get-tuple-element.216), channel_id=1, replica_groups=mesh['dp'=8,'space'=4] {'space'}, use_global_device_ids=true, to_apply=%region_61.62 | all-reduce | flops 3456 | bytes 27648 | tf_op jit(solution)/shard_map/psum | solution.py:159
  862.8 35.0 %all-reduce.5 = (f32[5,384]{1,0:T(8,128)S(1)}, f32[1536]{0:T(1024)}) all-reduce(f32[5,384]{1,0:T(8,128)} %get-tuple-element.185, f32[1536]{0:T(1024)} %get-tuple-element.186), channel_id=1, replica_groups=mesh['dp'=8,'space'=4] {'dp'}, use_global_device_ids=true, to_apply=%region_62.63 | all-reduce | flops 3456 | bytes 27648 | tf_op jit(solution)/shard_map/psum | solution.py:158
  902.0 4.3 copy.167
  906.3 2.9 multiply_reduce_fusion.5
  909.2 2.9 multiply_reduce_fusion.6
  (341 shorter events, 42.1 us)
Async XLA Ops:
  7.2 52.6 %copy-start.68 = (f32[5,12]{1,0:T(8,128)S(1)}, f32[5,12]{1,0:T(8,128)}, u32[]{:S(2)}) copy-start(f32[5,12]{1,0:T(8,128)} %param.26) | copy-start | bytes 724
  7.2 119.4 %copy-start.17 = (f32[49,12]{0,1:T(8,128)S(1)}, f32[49,12]{0,1:T(8,128)}, u32[]{:S(2)}) copy-start(f32[49,12]{0,1:T(8,128)} %param.23) | copy-start | bytes 7060
  7.2 164.1 %copy-start.107 = (f32[48]{0:T(128)S(1)}, f32[48]{0:T(128)}, u32[]{:S(2)}) copy-start(f32[48]{0:T(128)} %param.32) | copy-start | bytes 580
  7.2 44.6 %all-to-all-start = ((bf16[32,6,24,384]{3,2,1,0:T(8,128)(2,1)}), bf16[32,6,24,384]{3,2,1,0:T(8,128)(2,1)S(1)}, u32[]{:S(2)}, u32[]{:S(2)}) async-start(bf16[32,6,24,384]{3,2,1,0:T(8,128)(2,1)} %param.19), calls=%async_computation | async-start | bytes 7077888 | tf_op jit(solution)/shard_map/all_to_all | solution.py:89
  11.6 290.5 %all-gather.5.cloned.1.call-start = ((), (), s32[]{:S(2)}) async-start(), calls=%async_computation.4 | async-start | bytes 1216512 | tf_op jit(solution)/shard_map/all_gather | solution.py:79
  51.9 74.8 %copy-start.4 = (bf16[32,6,24,384]{3,2,1,0:T(8,128)(2,1)}, bf16[32,6,24,384]{3,2,1,0:T(8,128)(2,1)S(1)}, u32[]{:S(2)}) copy-start(bf16[32,6,24,384]{3,2,1,0:T(8,128)(2,1)S(1)} %all-to-all-done) | copy-start | bytes 10616836
  51.9 176.8 %all-to-all-start.2 = ((bf16[32,6,24,384]{3,2,1,0:T(8,128)(2,1)}), bf16[32,6,24,384]{3,2,1,0:T(8,128)(2,1)}, u32[]{:S(2)}, u32[]{:S(2)}) async-start(bf16[32,6,24,384]{3,2,1,0:T(8,128)(2,1)} %param.20), calls=%async_computation.2 | async-start | bytes 7077888 | tf_op jit(solution)/shard_map/all_to_all | solution.py:90
  58.2 262.5 %all-gather.7.cloned.1.call-start = ((), (), s32[]{:S(2)}) async-start(), calls=%async_computation.5 | async-start | bytes 1216512 | tf_op jit(solution)/shard_map/all_gather | solution.py:80
  59.8 561.1 %all-reduce.14.cloned.1.call-start = ((), (), s32[]{:S(2)}) async-start(), calls=%async_computation.7 | async-start | bytes 9830400 | tf_op jit(solution)/shard_map/psum | solution.py:159
  171.3 56.9 %copy-start.111 = (s32[8]{0:T(128)}, s32[8]{0:T(128)S(1)}, u32[]{:S(2)}) copy-start(s32[8]{0:T(128)S(1)} %dynamic_slice.21) | copy-start | bytes 100
  235.8 61.2 %copy-start = (bf16[8,30,24,384]{3,2,1,0:T(8,128)(2,1)}, bf16[8,30,24,384]{3,2,1,0:T(8,128)(2,1)S(1)}, u32[]{:S(2)}) copy-start(bf16[8,30,24,384]{3,2,1,0:T(8,128)(2,1)S(1)} %pad.17) | copy-start | bytes 13271044
  403.5 36.5 %copy-start.3 = (bf16[8,24,24,384]{3,2,1,0:T(8,128)(2,1)S(1)}, bf16[8,24,24,384]{3,2,1,0:T(8,128)(2,1)}, u32[]{:S(2)}) copy-start(bf16[8,24,24,384]{3,2,1,0:T(8,128)(2,1)} %copy-done.2) | copy-start | bytes 10616836
  457.0 32.9 %copy-start.79 = (f32[384]{0:T(512)S(1)}, f32[384]{0:T(512)}, u32[]{:S(2)}) copy-start(f32[384]{0:T(512)} %get-tuple-element.82) | copy-start | bytes 4612
  457.0 32.9 %copy-start.78 = (f32[384]{0:T(512)S(1)}, f32[384]{0:T(512)}, u32[]{:S(2)}) copy-start(f32[384]{0:T(512)} %get-tuple-element.83) | copy-start | bytes 4612
  457.1 32.9 %copy-start.77 = (f32[384]{0:T(512)S(1)}, f32[384]{0:T(512)}, u32[]{:S(2)}) copy-start(f32[384]{0:T(512)} %get-tuple-element.84) | copy-start | bytes 4612
  457.1 32.9 %copy-start.76 = (f32[384]{0:T(512)S(1)}, f32[384]{0:T(512)}, u32[]{:S(2)}) copy-start(f32[384]{0:T(512)} %get-tuple-element.85) | copy-start | bytes 4612
  457.1 32.9 %copy-start.75 = (f32[384]{0:T(512)S(1)}, f32[384]{0:T(512)}, u32[]{:S(2)}) copy-start(f32[384]{0:T(512)} %get-tuple-element.86) | copy-start | bytes 4612
  457.1 32.9 %copy-start.74 = (f32[384]{0:T(512)S(1)}, f32[384]{0:T(512)}, u32[]{:S(2)}) copy-start(f32[384]{0:T(512)} %get-tuple-element.87) | copy-start | bytes 4612
  457.1 32.9 %copy-start.73 = (f32[384]{0:T(512)S(1)}, f32[384]{0:T(512)}, u32[]{:S(2)}) copy-start(f32[384]{0:T(512)} %get-tuple-element.88) | copy-start | bytes 4612
  457.1 33.0 %copy-start.97 = (f32[384]{0:T(512)S(1)}, f32[384]{0:T(512)}, u32[]{:S(2)}) copy-start(f32[384]{0:T(512)} %get-tuple-element.117) | copy-start | bytes 4612
  457.1 33.0 %copy-start.96 = (f32[384]{0:T(512)S(1)}, f32[384]{0:T(512)}, u32[]{:S(2)}) copy-start(f32[384]{0:T(512)} %get-tuple-element.118) | copy-start | bytes 4612
  457.1 33.0 %copy-start.95 = (f32[384]{0:T(512)S(1)}, f32[384]{0:T(512)}, u32[]{:S(2)}) copy-start(f32[384]{0:T(512)} %get-tuple-element.119) | copy-start | bytes 4612
  457.1 33.0 %copy-start.94 = (f32[384]{0:T(512)S(1)}, f32[384]{0:T(512)}, u32[]{:S(2)}) copy-start(f32[384]{0:T(512)} %get-tuple-element.120) | copy-start | bytes 4612
  457.1 33.0 %copy-start.93 = (f32[384]{0:T(512)S(1)}, f32[384]{0:T(512)}, u32[]{:S(2)}) copy-start(f32[384]{0:T(512)} %get-tuple-element.121) | copy-start | bytes 4612
  457.2 33.0 %copy-start.92 = (f32[384]{0:T(512)S(1)}, f32[384]{0:T(512)}, u32[]{:S(2)}) copy-start(f32[384]{0:T(512)} %get-tuple-element.122) | copy-start | bytes 4612
  501.5 119.3 %copy-start.22 = (f32[384]{0:T(512)S(1)}, f32[384]{0:T(512)}, u32[]{:S(2)}) copy-start(f32[384]{0:T(512)} %copy-done.21) | copy-start | bytes 4612
  501.5 119.3 %copy-start.24 = (f32[384]{0:T(512)S(1)}, f32[384]{0:T(512)}, u32[]{:S(2)}) copy-start(f32[384]{0:T(512)} %copy-done.23) | copy-start | bytes 4612
  501.5 119.3 %copy-start.26 = (f32[384]{0:T(512)S(1)}, f32[384]{0:T(512)}, u32[]{:S(2)}) copy-start(f32[384]{0:T(512)} %copy-done.25) | copy-start | bytes 4612
  501.5 119.3 %copy-start.28 = (f32[384]{0:T(512)S(1)}, f32[384]{0:T(512)}, u32[]{:S(2)}) copy-start(f32[384]{0:T(512)} %copy-done.27) | copy-start | bytes 4612
  501.5 307.9 %all-to-all-start.1 = ((bf16[8,24,24,384]{3,2,0,1:T(8,128)(2,1)}), bf16[8,24,24,384]{3,2,0,1:T(8,128)(2,1)S(1)}, u32[]{:S(2)}, u32[]{:S(2)}) async-start(bf16[8,24,24,384]{3,2,0,1:T(8,128)(2,1)} %copy.163), calls=%async_computation.1 | async-start | bytes 7077888 | tf_op jit(solution)/shard_map/all_to_all | solution.py:154
  505.3 401.0 %all-reduce.12.cloned.1.call-start = ((), (), s32[]{:S(2)}) async-start(), calls=%async_computation.6 | async-start | bytes 9830400 | tf_op jit(solution)/shard_map/psum | solution.py:158
  809.4 92.6 %all-to-all-start.3 = ((bf16[8,24,24,384]{3,2,0,1:T(8,128)(2,1)}), bf16[8,24,24,384]{3,2,0,1:T(8,128)(2,1)}, u32[]{:S(2)}, u32[]{:S(2)}) async-start(bf16[8,24,24,384]{3,2,0,1:T(8,128)(2,1)} %copy.166), calls=%async_computation.3 | async-start | bytes 7077888 | tf_op jit(solution)/shard_map/all_to_all | solution.py:155
  (93 other events, 984.1 us)
Sparse Core Ops, SparseCore 0:
  15.9 54.4 all-gather.4
  73.9 53.8 all-gather.6
  491.6 129.1 all-reduce.13
  625.2 174.4 all-reduce.11
